TPU v7x, 128 devices: a whole 4x4x4 slice. The times are simulated.
128 devices in a mesh: gx: 8 (over z, x_lo), gy: 16 (over x_hi, y, core).
Axes of the slice: x: 4 (x_hi: 2, x_lo: 2; x = x_hi * 2 + x_lo), y: 4, z: 4, core: 2. Of those that a mesh axis runs over, the one named last changes fastest.
Arguments:
- fields: float32 [6, 256, 512, 128], P(None, 'gx', 'gy'), may hold values from -6 to 6
- eps_background: float32 [256, 512, 128], P('gx', 'gy'), may hold values from 1 to 4
- target: float32 [256, 256], replicated, may hold values from 1 to 10
- widths: float32 [16384], P(('gx', 'gy')), may hold values from 0.2 to 1
- intersection: float32 [16384, 16], P(('gx', 'gy')), may hold values from 0.1 to 1
- pillar_tile: int32 [16384, 1], P(('gx', 'gy')), may hold values from 0 to 127; in each aligned block of 128 rows (0 to 127, 128 to 255, ...) at most 2 rows name the same one
- anchors: int32 [16384, 2], P(('gx', 'gy')), may hold values from 0 to 28
Outputs:
- final_fields: float32 [6, 256, 512, 128], P(None, 'gx', 'gy')
- focal_power: float32 [256, 256], P(('gx', 'gy'))
- grad_widths: float32 [16384], P(('gx', 'gy'))
Inputs may be any that keep to these rules, and one draw needn't show every extreme that they name: `pillar_tile`: in the pillars of one device (aligned blocks of 128), no tile is named by more than 2 pillars, a bound that some block reaches. Tile t is the one at gx index t div (512 div 32) and gy index t mod (512 div 32).
All inputs are finite; a program needn't handle non-finite values.
Results may differ from a plain program's by a relative error of at most 0.00016.
Values sent between devices are 32-bit elements; how exact they have to be, the bound alone decides.
A program may use at most 128 MiB of HBM per device.

v0:
```python
import math
import jax
import jax.numpy as jnp
from jax import lax
from jax.sharding import PartitionSpec as P

TILE = 32
P_DEV = 128
NT = 4
ZP = 4
U = 256
V = 256
ZM = 64
COURANT = 0.5
ANGULAR_STEP = 0.9
DELTA_EPS = 4.0


def passed_along(shard, axis, by):
    count = lax.axis_size(axis)
    pairs = [(i, i + by) for i in range(count) if 0 <= i + by < count]
    return lax.ppermute(shard, axis, pairs)


def plus_diff(field, rim_layer, axis):
    extended = jnp.concatenate([field, rim_layer], axis=axis)
    return lax.slice_in_dim(extended, 1, extended.shape[axis], axis=axis) - field


def minus_diff(field, rim_layer, axis):
    extended = jnp.concatenate([rim_layer, field], axis=axis)
    return field - lax.slice_in_dim(extended, 0, field.shape[axis], axis=axis)


def leap_step(fields_now, inv_eps, sources):
    elec_x, elec_y, elec_z, magn_x, magn_y, magn_z = fields_now
    z_blank = jnp.zeros_like(elec_x[:, :, :1])
    rim_east = passed_along(jnp.stack([elec_y[:1], elec_z[:1]]), "gx", -1)
    rim_north = passed_along(jnp.stack([elec_x[:, :1], elec_z[:, :1]]), "gy", -1)
    curl_x = plus_diff(elec_z, rim_north[1], 1) - plus_diff(elec_y, z_blank, 2)
    curl_y = plus_diff(elec_x, z_blank, 2) - plus_diff(elec_z, rim_east[1], 0)
    curl_z = plus_diff(elec_y, rim_east[0], 0) - plus_diff(elec_x, rim_north[0], 1)
    magn_x = magn_x - COURANT * curl_x
    magn_y = magn_y - COURANT * curl_y
    magn_z = magn_z - COURANT * curl_z
    rim_west = passed_along(jnp.stack([magn_y[-1:], magn_z[-1:]]), "gx", 1)
    rim_south = passed_along(jnp.stack([magn_x[:, -1:], magn_z[:, -1:]]), "gy", 1)
    curl_x = minus_diff(magn_z, rim_south[1], 1) - minus_diff(magn_y, z_blank, 2)
    curl_y = minus_diff(magn_x, z_blank, 2) - minus_diff(magn_z, rim_west[1], 0)
    curl_z = minus_diff(magn_y, rim_west[0], 0) - minus_diff(magn_x, rim_south[0], 1)
    elec_x = elec_x + COURANT * (curl_x - sources[0]) * inv_eps
    elec_y = elec_y + COURANT * (curl_y - sources[1]) * inv_eps
    elec_z = elec_z + COURANT * curl_z * inv_eps
    return (elec_x, elec_y, elec_z, magn_x, magn_y, magn_z)


def kernel_table(count_out, count_in, offset, length):
    focal_pos = (jnp.arange(count_out, dtype=jnp.float32) + 0.5) / count_out - 0.5
    cell_pos = (
        offset.astype(jnp.float32) + jnp.arange(length, dtype=jnp.float32) + 0.5
    ) / count_in - 0.5
    phase = math.pi * count_out * (focal_pos[:, None] - cell_pos[None, :]) ** 2
    return (jnp.cos(phase), jnp.sin(phase))


def contract(pattern, first_op, second_op):
    return jnp.einsum(pattern, first_op, second_op, precision=lax.Precision.HIGHEST)


def project_forward(mon_re, mon_im, table_x, table_y, norm_scale):
    x_re, x_im = table_x
    y_re, y_im = table_y
    part_re = contract("ux,cxy->cuy", x_re, mon_re) - contract("ux,cxy->cuy", x_im, mon_im)
    part_im = contract("ux,cxy->cuy", x_re, mon_im) + contract("ux,cxy->cuy", x_im, mon_re)
    far_re = contract("cuy,vy->cuv", part_re, y_re) - contract("cuy,vy->cuv", part_im, y_im)
    far_im = contract("cuy,vy->cuv", part_re, y_im) + contract("cuy,vy->cuv", part_im, y_re)
    return norm_scale * jnp.stack([far_re, far_im])


def project_back(weighted, table_x, table_y, norm_scale):
    x_re, x_im = table_x
    y_re, y_im = table_y
    w_re = weighted[0]
    w_im = weighted[1]
    half_re = contract("cuv,vy->cuy", w_re, y_re) - contract("cuv,vy->cuy", w_im, y_im)
    half_im = contract("cuv,vy->cuy", w_re, y_im) + contract("cuv,vy->cuy", w_im, y_re)
    back_re = contract("ux,cuy->cxy", x_re, half_re) - contract("ux,cuy->cxy", x_im, half_im)
    back_im = contract("ux,cuy->cxy", x_re, half_im) + contract("ux,cuy->cxy", x_im, half_re)
    return (2.0 * norm_scale * back_re, 2.0 * norm_scale * back_im)


def shards(fields, eps_background, target, widths, intersection, pillar_tile, anchors):
    span_x = lax.axis_size("gx")
    span_y = lax.axis_size("gy")
    devices = span_x * span_y
    place_x = lax.axis_index("gx")
    place_y = lax.axis_index("gy")
    linear = place_x * span_y + place_y
    offsets = jnp.arange(16, dtype=jnp.int32)
    capacity = 2 * max(1, P_DEV // devices)
    target_tile = pillar_tile[:, 0]
    onehot = (target_tile[:, None] == jnp.arange(devices, dtype=jnp.int32)[None, :]).astype(
        jnp.int32
    )
    earlier = jnp.cumsum(onehot, axis=0) - onehot
    order_in = jnp.sum(earlier * onehot, axis=1)
    slot_ids = target_tile * capacity + order_in
    packed = (
        jnp.zeros((devices * capacity, 16), jnp.float32)
        .at[slot_ids]
        .set(intersection * widths[:, None])
    )
    packed_at = (
        jnp.zeros((devices * capacity, 2), jnp.float32)
        .at[slot_ids]
        .set(anchors.astype(jnp.float32))
    )
    got_vals, got_at = (
        lax.all_to_all(
            packed.reshape(devices, capacity, 16),
            ("gx", "gy"),
            split_axis=0,
            concat_axis=0,
            tiled=True,
        ),
        lax.all_to_all(
            packed_at.reshape(devices, capacity, 2),
            ("gx", "gy"),
            split_axis=0,
            concat_axis=0,
            tiled=True,
        ),
    )
    local_vals = got_vals.reshape(devices * capacity, 16)
    local_at = got_at.reshape(devices * capacity, 2).astype(jnp.int32)
    cells_x = local_at[:, 0:1] + (offsets // 4)[None, :]
    cells_y = local_at[:, 1:2] + (offsets % 4)[None, :]
    filling = jnp.zeros((TILE, TILE), jnp.float32).at[cells_x, cells_y].add(local_vals)
    z_index = jnp.arange(fields.shape[3], dtype=jnp.int32)
    layers = ((z_index >= ZM - ZP) & (z_index < ZM)).astype(jnp.float32)
    permittivity = eps_background + DELTA_EPS * filling[:, :, None] * layers[None, None, :]
    inv_eps = 1.0 / permittivity
    blank = jnp.zeros_like(eps_background)
    fields_now = tuple((fields[component] for component in range(6)))
    mon_re = jnp.zeros((2, TILE, TILE), jnp.float32)
    mon_im = jnp.zeros((2, TILE, TILE), jnp.float32)
    changes = []
    for moment in range(1, NT + 1):
        before = fields_now[:3]
        fields_now = leap_step(fields_now, inv_eps, (blank, blank, blank))
        monitor = jnp.stack([fields_now[0][:, :, ZM], fields_now[1][:, :, ZM]])
        mon_re = mon_re + math.cos(ANGULAR_STEP * moment) * monitor
        mon_im = mon_im - math.sin(ANGULAR_STEP * moment) * monitor
        changes.append(
            tuple(
                (
                    (fields_now[component] - before[component])[:, :, ZM - ZP : ZM]
                    for component in range(3)
                )
            )
        )
    norm_scale = (TILE * span_x * TILE * span_y) ** (-0.5)
    table_x = kernel_table(U, TILE * span_x, place_x * TILE, TILE)
    table_y = kernel_table(V, TILE * span_y, place_y * TILE, TILE)
    row_count = U // devices
    row_start = linear * row_count
    partial_far = project_forward(mon_re, mon_im, table_x, table_y, norm_scale)
    far_field = lax.psum(partial_far, ("gx", "gy"))
    mine_rows = lax.dynamic_slice_in_dim(far_field, row_start, row_count, 2)
    focal_power = jnp.sum(mine_rows * mine_rows, axis=(0, 1))
    weighted = jnp.stack([target * far_field[0], -(target * far_field[1])])
    back_re, back_im = project_back(weighted, table_x, table_y, norm_scale)
    adjoint = tuple((blank for component in range(6)))
    inv_layer = inv_eps[:, :, ZM - ZP : ZM]
    grad_eps = jnp.zeros((TILE, TILE, ZP), jnp.float32)
    for moment in range(1, NT + 1):
        source_step = NT + 1 - moment
        adj_drive = (
            math.cos(ANGULAR_STEP * source_step) * back_re
            + math.sin(ANGULAR_STEP * source_step) * back_im
        )
        source_x = blank.at[:, :, ZM].set(adj_drive[0])
        source_y = blank.at[:, :, ZM].set(adj_drive[1])
        adjoint = leap_step(adjoint, inv_eps, (source_x, source_y, blank))
        change = changes[source_step - 1]
        product = (
            adjoint[0][:, :, ZM - ZP : ZM] * change[0]
            + adjoint[1][:, :, ZM - ZP : ZM] * change[1]
            + adjoint[2][:, :, ZM - ZP : ZM] * change[2]
        )
        grad_eps = grad_eps - product * inv_layer
    column_grad = jnp.sum(grad_eps, axis=2)
    picked = column_grad[cells_x, cells_y]
    returned = lax.all_to_all(
        picked.reshape(devices, capacity, 16), ("gx", "gy"), split_axis=0, concat_axis=0, tiled=True
    )
    own_vals = returned.reshape(devices * capacity, 16)[slot_ids]
    grad_widths = DELTA_EPS * jnp.sum(intersection * own_vals, axis=1)
    return (jnp.stack(fields_now), focal_power, grad_widths)


def solution(mesh):
    placed = (
        P(None, "gx", "gy", None),
        P("gx", "gy", None),
        P(),
        P(("gx", "gy")),
        P(("gx", "gy"), None),
        P(("gx", "gy"), None),
        P(("gx", "gy"), None),
    )
    return jax.shard_map(
        shards,
        mesh=mesh,
        in_specs=placed,
        out_specs=(P(None, "gx", "gy", None), P(("gx", "gy"), None), P(("gx", "gy"))),
        check_vma=False,
    )
```

profile of v0, /device:TPU:1, one launch (start us, length us, event | category | flops | bytes accessed | tf_op | source)
XLA Modules:
  0.0 479.0 jit_solution(2018501460073034488)
XLA Ops:
  7.2 1.6 collective-permute-start.16
  9.4 3.3 collective-permute-start.17
  16.8 1.5 copy.4958
  18.3 12.4 %all-to-all-start = ((f32[128,2,2]{1,2,0:T(2,128)}), f32[128,2,2]{1,2,0:T(2,128)S(1)}, u32[]{:S(2)}, u32[]{:S(2)}) async-start(f32[128,2,2]{1,2,0:T(2,128)} %copy.4958), calls=%async_computation | async-start | bytes 262144 | tf_op jit(solution)/shard_map/all_to_all | solution.py:126
  30.7 2.3 slice_bitcast_fusion.3
  34.6 3.0 collective-permute-start.1
  42.3 11.5 %all-to-all-start.1 = ((f32[128,2,16]{2,1,0:T(2,128)}), f32[128,2,16]{2,1,0:T(2,128)S(1)}, u32[]{:S(2)}, u32[]{:S(2)}) async-start(f32[128,2,16]{2,1,0:T(2,128)} %bitcast.24), calls=%async_computation.1 | async-start | bytes 262144 | tf_op jit(solution)/shard_map/all_to_all | solution.py:119
  56.7 7.2 %all-to-all-done.1 = f32[128,2,16]{2,1,0:T(2,128)S(1)} async-done(((f32[128,2,16]{2,1,0:T(2,128)}), f32[128,2,16]{2,1,0:T(2,128)S(1)}, u32[]{:S(2)}, u32[]{:S(2)}) %all-to-all-start.1) | async-done | bytes 16416 | tf_op jit(solution)/shard_map/all_to_all | solution.py:119
  64.0 28.9 %scatter_custom_fusion.2 = f32[1024]{0:T(1024)S(1)} fusion(s32[4096]{0:T(1024)} %reshape.500, f32[4096]{0:T(1024)S(1)} %reshape.502, f32[]{:T(128)} %constant.251.clone.1), kind=kCustom, calls=%fused_computation.635 | custom fusion | flops 4096 | bytes 4608
  95.3 2.7 collective-permute-start.18
  98.0 2.2 collective-permute-start.19
  102.4 3.5 collective-permute-start.3
  105.9 2.6 collective-permute-start.2
  111.5 1.9 collective-permute-start.5
  116.8 2.6 collective-permute-done.4
  120.0 3.1 collective-permute-start.7
  123.1 5.1 %collective-permute-start.6 = (f32[2,32,1,128]{3,1,2,0:T(8,128)S(1)}, f32[2,32,1,128]{3,1,2,0:T(8,128)S(1)}, u32[]{:S(2)}, u32[]{:S(2)}) collective-permute-start(f32[2,32,1,128]{3,1,2,0:T(8,128)S(1)} %pad_maximum_fusion.63), channel_id=1, source_target_pairs={{0,1},{1,2},{2,3},{3,4},{4,5},{5,6},{6,7},{7,8},{8,9},{9,10},{10,1... | collective-permute-start | bytes 98312 | tf_op jit(solution)/shard_map/ppermute | solution.py:22
  130.7 1.9 collective-permute-start.9
  133.9 2.6 collective-permute-done.9
  137.9 2.7 collective-permute-start.11
  140.7 5.8 %collective-permute-start.10 = (f32[2,32,1,128]{3,1,2,0:T(8,128)S(1)}, f32[2,32,1,128]{3,1,2,0:T(8,128)S(1)}, u32[]{:S(2)}, u32[]{:S(2)}) collective-permute-start(f32[2,32,1,128]{3,1,2,0:T(8,128)S(1)} %pad_maximum_fusion.67), channel_id=1, source_target_pairs={{0,1},{1,2},{2,3},{3,4},{4,5},{5,6},{6,7},{7,8},{8,9},{9,10},{10,1... | collective-permute-start | bytes 98312 | tf_op jit(solution)/shard_map/ppermute | solution.py:22
  148.8 1.9 collective-permute-start.13
  152.0 2.6 collective-permute-done.13
  156.1 5.4 %collective-permute-start.14 = (f32[2,32,1,128]{3,1,2,0:T(8,128)S(1)}, f32[2,32,1,128]{3,1,2,0:T(8,128)S(1)}, u32[]{:S(2)}, u32[]{:S(2)}) collective-permute-start(f32[2,32,1,128]{3,1,2,0:T(8,128)S(1)} %pad_maximum_fusion.71), channel_id=1, source_target_pairs={{0,1},{1,2},{2,3},{3,4},{4,5},{5,6},{6,7},{7,8},{8,9},{9,10},{10,1... | collective-permute-start | bytes 98312 | tf_op jit(solution)/shard_map/ppermute | solution.py:22
  161.5 3.1 collective-permute-start.15
  173.1 3.1 bitcast_dynamic-update-slice_fusion.3
  177.8 152.3 %all-reduce.45.cloned.1.call-done = f32[2,2,256,256]{3,2,1,0:T(8,128)} async-done(((f32[2,2,256,256]{3,2,1,0:T(8,128)}), f32[2,2,256,256]{3,2,1,0:T(8,128)}) %all-reduce.45.cloned.1.call-update) | async-done | bytes 1048592 | tf_op jit(solution)/shard_map/psum | solution.py:168
  330.2 1.8 fusion.284
  332.0 1.8 convolution_add_fusion.2
  334.2 1.8 fusion.286
  335.9 1.8 convolution_subtract_fusion.2
  341.5 3.0 fusion.94
  344.5 1.9 collective-permute-start.21
  356.4 4.0 fusion.98
  360.5 4.0 collective-permute-start.23
  364.5 4.2 collective-permute-start.22
  370.7 2.1 collective-permute-start.25
  374.1 2.6 collective-permute-done.25
  378.1 4.0 collective-permute-start.27
  382.2 5.7 %collective-permute-start.26 = (f32[2,32,1,128]{3,1,2,0:T(8,128)S(1)}, f32[2,32,1,128]{3,1,2,0:T(8,128)S(1)}, u32[]{:S(2)}, u32[]{:S(2)}) collective-permute-start(f32[2,32,1,128]{3,1,2,0:T(8,128)S(1)} %pad_maximum_fusion.85), channel_id=1, source_target_pairs={{0,1},{1,2},{2,3},{3,4},{4,5},{5,6},{6,7},{7,8},{8,9},{9,10},{10,1... | collective-permute-start | bytes 98312 | tf_op jit(solution)/shard_map/ppermute | solution.py:22
  389.8 1.9 collective-permute-start.29
  393.0 2.6 collective-permute-done.29
  397.6 2.7 collective-permute-start.31
  400.3 5.7 %collective-permute-start.30 = (f32[2,32,1,128]{3,1,2,0:T(8,128)S(1)}, f32[2,32,1,128]{3,1,2,0:T(8,128)S(1)}, u32[]{:S(2)}, u32[]{:S(2)}) collective-permute-start(f32[2,32,1,128]{3,1,2,0:T(8,128)S(1)} %pad_maximum_fusion.89), channel_id=1, source_target_pairs={{0,1},{1,2},{2,3},{3,4},{4,5},{5,6},{6,7},{7,8},{8,9},{9,10},{10,1... | collective-permute-start | bytes 98312 | tf_op jit(solution)/shard_map/ppermute | solution.py:22
  407.0 5.4 %fusion.147 = f32[32,32]{1,0:T(8,128)S(1)} fusion(f32[32,32,128]{2,1,0:T(8,128)S(1)} %copy-done.26, f32[32,32,128]{2,1,0:T(8,128)S(1)} %get-tuple-element.164, f32[1,32,128]{2,1,0:T(8,128)S(1)} %get-tuple-element.191, f32[32,32,128]{2,1,0:T(8,128)S(1)} %get-tuple-element.163, f32[32,1,128]{2,1,0:T(1,128)S(1)} %bitcast.473, ...), kind=kLoop, calls=%fused_computation.197 | loop fusion | flops 265216 | bytes 18419712 | tf_op jit(solution)/shard_map/reduce_sum | solution.py:192
  412.5 27.6 %gather_fusion = f32[4096]{0:T(1024)S(1)} fusion(f32[32,32]{0,1:T(8,128)S(1)} %copy.5037, s32[4096]{0:T(1024)S(1)} %reshape.470), kind=kCustom, calls=%fused_computation | custom fusion | bytes 65536 | tf_op jit(solution)/shard_map/gather | solution.py:193
  441.0 19.8 %all-to-all-start.2 = ((f32[128,2,16]{2,1,0:T(2,128)}), f32[128,2,16]{2,1,0:T(2,128)S(1)}, u32[]{:S(2)}, u32[]{:S(2)}) async-start(f32[128,2,16]{2,1,0:T(2,128)} %reshape.462), calls=%async_computation.2 | async-start | bytes 262144 | tf_op jit(solution)/shard_map/all_to_all | solution.py:194
  463.0 8.0 %all-to-all-done.2 = f32[128,2,16]{2,1,0:T(2,128)S(1)} async-done(((f32[128,2,16]{2,1,0:T(2,128)}), f32[128,2,16]{2,1,0:T(2,128)S(1)}, u32[]{:S(2)}, u32[]{:S(2)}) %all-to-all-start.2) | async-done | bytes 16416 | tf_op jit(solution)/shard_map/all_to_all | solution.py:194
  (362 shorter events, 74.2 us)
Async XLA Ops:
  7.2 30.4 %copy-start.20 = (f32[6,32,32,128]{3,2,1,0:T(8,128)S(1)}, f32[6,32,32,128]{3,2,1,0:T(8,128)}, u32[]{:S(2)}) copy-start(f32[6,32,32,128]{3,2,1,0:T(8,128)} %param.23) | copy-start | bytes 9437188
  7.2 33.3 %copy-start.52 = (f32[128,16]{0,1:T(8,128)S(1)}, f32[128,16]{0,1:T(8,128)}, u32[]{:S(2)}) copy-start(f32[128,16]{0,1:T(8,128)} %param.27) | copy-start | bytes 24580
  7.2 33.3 %copy-start.54 = (f32[128]{0:T(128)S(1)}, f32[128]{0:T(128)}, u32[]{:S(2)}) copy-start(f32[128]{0:T(128)} %param.26) | copy-start | bytes 1540
  7.2 85.9 %collective-permute-start.16 = (f32[2,1,32,128]{3,2,1,0:T(8,128)S(1)}, f32[2,1,32,128]{3,2,1,0:T(8,128)}, u32[]{:S(2)}, u32[]{:S(2)}) collective-permute-start(f32[2,1,32,128]{3,2,1,0:T(8,128)S(1)} %stack.374), channel_id=1, source_target_pairs={{16,0},{32,16},{48,32},{64,48},{80,64},{96,80},{112,96},{17,1},{33... | collective-permute-start | bytes 98312 | tf_op jit(solution)/shard_map/ppermute | solution.py:22
  9.4 84.6 %collective-permute-start.17 = (f32[2,32,1,128]{3,1,2,0:T(8,128)}, f32[2,32,1,128]{3,1,2,0:T(8,128)}, u32[]{:S(2)}, u32[]{:S(2)}) collective-permute-start(f32[2,32,1,128]{3,1,2,0:T(8,128)} %stack.375), channel_id=1, source_target_pairs={{1,0},{2,1},{3,2},{4,3},{5,4},{6,5},{7,6},{8,7},{9,8},{10,9},{11,1... | collective-permute-start | bytes 98312 | tf_op jit(solution)/shard_map/ppermute | solution.py:22
  18.3 23.9 %all-to-all-start = ((f32[128,2,2]{1,2,0:T(2,128)}), f32[128,2,2]{1,2,0:T(2,128)S(1)}, u32[]{:S(2)}, u32[]{:S(2)}) async-start(f32[128,2,2]{1,2,0:T(2,128)} %copy.4958), calls=%async_computation | async-start | bytes 262144 | tf_op jit(solution)/shard_map/all_to_all | solution.py:126
  34.6 65.6 %collective-permute-start.1 = (f32[2,32,1,128]{3,1,2,0:T(8,128)}, f32[2,32,1,128]{3,1,2,0:T(8,128)}, u32[]{:S(2)}, u32[]{:S(2)}) collective-permute-start(f32[2,32,1,128]{3,1,2,0:T(8,128)} %pad_maximum_fusion.58), channel_id=1, source_target_pairs={{1,0},{2,1},{3,2},{4,3},{5,4},{6,5},{7,6},{8,7},{9,8},{10,9},{11,1... | collective-permute-start | bytes 98312 | tf_op jit(solution)/shard_map/ppermute | solution.py:22
  38.1 62.8 %collective-permute-start = (f32[2,1,32,128]{3,2,1,0:T(8,128)}, f32[2,1,32,128]{3,2,1,0:T(8,128)}, u32[]{:S(2)}, u32[]{:S(2)}) collective-permute-start(f32[2,1,32,128]{3,2,1,0:T(8,128)} %stack.314), channel_id=1, source_target_pairs={{16,0},{32,16},{48,32},{64,48},{80,64},{96,80},{112,96},{17,1},{33... | collective-permute-start | bytes 98312 | tf_op jit(solution)/shard_map/ppermute | solution.py:22
  42.3 21.6 %all-to-all-start.1 = ((f32[128,2,16]{2,1,0:T(2,128)}), f32[128,2,16]{2,1,0:T(2,128)S(1)}, u32[]{:S(2)}, u32[]{:S(2)}) async-start(f32[128,2,16]{2,1,0:T(2,128)} %bitcast.24), calls=%async_computation.1 | async-start | bytes 262144 | tf_op jit(solution)/shard_map/all_to_all | solution.py:119
  53.7 276.5 %all-reduce.45.cloned.1.call-start = ((), (), s32[]{:S(2)}) async-start(), calls=%async_computation.3 | async-start | bytes 2097152 | tf_op jit(solution)/shard_map/psum | solution.py:168
  95.2 14.8 %copy-start.22 = (f32[32,32,128]{2,1,0:T(8,128)}, f32[32,32,128]{2,1,0:T(8,128)S(1)}, u32[]{:S(2)}) copy-start(f32[32,32,128]{2,1,0:T(8,128)S(1)} %get-tuple-element.179) | copy-start | bytes 1572868
  95.3 13.2 %collective-permute-start.18 = (f32[2,32,1,128]{3,1,2,0:T(8,128)S(1)}, f32[2,32,1,128]{3,1,2,0:T(8,128)S(1)}, u32[]{:S(2)}, u32[]{:S(2)}) collective-permute-start(f32[2,32,1,128]{3,1,2,0:T(8,128)S(1)} %pad_maximum_fusion.77), channel_id=1, source_target_pairs={{0,1},{1,2},{2,3},{3,4},{4,5},{5,6},{6,7},{7,8},{8,9},{9,10},{10,1... | collective-permute-start | bytes 98312 | tf_op jit(solution)/shard_map/ppermute | solution.py:22
  98.0 11.2 %collective-permute-start.19 = (f32[2,1,32,128]{3,2,1,0:T(8,128)S(1)}, f32[2,1,32,128]{3,2,1,0:T(8,128)S(1)}, u32[]{:S(2)}, u32[]{:S(2)}) collective-permute-start(f32[2,1,32,128]{3,2,1,0:T(8,128)S(1)} %pad_maximum_fusion.78), channel_id=1, source_target_pairs={{0,16},{16,32},{32,48},{48,64},{64,80},{80,96},{96,112},{1,17},{17... | collective-permute-start | bytes 98312 | tf_op jit(solution)/shard_map/ppermute | solution.py:22
  102.4 7.7 %collective-permute-start.3 = (f32[2,1,32,128]{3,2,1,0:T(8,128)S(1)}, f32[2,1,32,128]{3,2,1,0:T(8,128)S(1)}, u32[]{:S(2)}, u32[]{:S(2)}) collective-permute-start(f32[2,1,32,128]{3,2,1,0:T(8,128)S(1)} %pad_maximum_fusion.60), channel_id=1, source_target_pairs={{0,16},{16,32},{32,48},{48,64},{64,80},{80,96},{96,112},{1,17},{17... | collective-permute-start | bytes 98312 | tf_op jit(solution)/shard_map/ppermute | solution.py:22
  105.9 4.2 collective-permute-start.2
  110.7 18.5 %copy-start.8 = (f32[32,32,128]{2,1,0:T(8,128)}, f32[32,32,128]{2,1,0:T(8,128)S(1)}, u32[]{:S(2)}) copy-start(f32[32,32,128]{2,1,0:T(8,128)S(1)} %get-tuple-element.138) | copy-start | bytes 1572868
  111.5 5.2 %collective-permute-start.5 = (f32[2,32,1,128]{3,1,2,0:T(8,128)S(1)}, f32[2,32,1,128]{3,1,2,0:T(8,128)S(1)}, u32[]{:S(2)}, u32[]{:S(2)}) collective-permute-start(f32[2,32,1,128]{3,1,2,0:T(8,128)S(1)} %pad_maximum_fusion.62), channel_id=1, source_target_pairs={{1,0},{2,1},{3,2},{4,3},{5,4},{6,5},{7,6},{8,7},{9,8},{10,9},{11,1... | collective-permute-start | bytes 98312 | tf_op jit(solution)/shard_map/ppermute | solution.py:22
  114.7 4.6 collective-permute-start.4
  120.0 8.2 %collective-permute-start.7 = (f32[2,1,32,128]{3,2,1,0:T(8,128)S(1)}, f32[2,1,32,128]{3,2,1,0:T(8,128)S(1)}, u32[]{:S(2)}, u32[]{:S(2)}) collective-permute-start(f32[2,1,32,128]{3,2,1,0:T(8,128)S(1)} %pad_maximum_fusion.64), channel_id=1, source_target_pairs={{0,16},{16,32},{32,48},{48,64},{64,80},{80,96},{96,112},{1,17},{17... | collective-permute-start | bytes 98312 | tf_op jit(solution)/shard_map/ppermute | solution.py:22
  123.1 6.1 %collective-permute-start.6 = (f32[2,32,1,128]{3,1,2,0:T(8,128)S(1)}, f32[2,32,1,128]{3,1,2,0:T(8,128)S(1)}, u32[]{:S(2)}, u32[]{:S(2)}) collective-permute-start(f32[2,32,1,128]{3,1,2,0:T(8,128)S(1)} %pad_maximum_fusion.63), channel_id=1, source_target_pairs={{0,1},{1,2},{2,3},{3,4},{4,5},{5,6},{6,7},{7,8},{8,9},{9,10},{10,1... | collective-permute-start | bytes 98312 | tf_op jit(solution)/shard_map/ppermute | solution.py:22
  129.8 17.5 %copy-start = (f32[32,32,128]{2,1,0:T(8,128)}, f32[32,32,128]{2,1,0:T(8,128)S(1)}, u32[]{:S(2)}) copy-start(f32[32,32,128]{2,1,0:T(8,128)S(1)} %get-tuple-element.162) | copy-start | bytes 1572868
  129.8 17.5 %copy-start.10 = (f32[32,32,128]{2,1,0:T(8,128)}, f32[32,32,128]{2,1,0:T(8,128)S(1)}, u32[]{:S(2)}) copy-start(f32[32,32,128]{2,1,0:T(8,128)S(1)} %get-tuple-element.161) | copy-start | bytes 1572868
  130.7 5.8 %collective-permute-start.9 = (f32[2,32,1,128]{3,1,2,0:T(8,128)S(1)}, f32[2,32,1,128]{3,1,2,0:T(8,128)S(1)}, u32[]{:S(2)}, u32[]{:S(2)}) collective-permute-start(f32[2,32,1,128]{3,1,2,0:T(8,128)S(1)} %pad_maximum_fusion.66), channel_id=1, source_target_pairs={{1,0},{2,1},{3,2},{4,3},{5,4},{6,5},{7,6},{8,7},{9,8},{10,9},{11,1... | collective-permute-start | bytes 98312 | tf_op jit(solution)/shard_map/ppermute | solution.py:22
  132.6 4.7 collective-permute-start.8
  137.9 8.6 %collective-permute-start.11 = (f32[2,1,32,128]{3,2,1,0:T(8,128)S(1)}, f32[2,1,32,128]{3,2,1,0:T(8,128)S(1)}, u32[]{:S(2)}, u32[]{:S(2)}) collective-permute-start(f32[2,1,32,128]{3,2,1,0:T(8,128)S(1)} %pad_maximum_fusion.68), channel_id=1, source_target_pairs={{0,16},{16,32},{32,48},{48,64},{64,80},{80,96},{96,112},{1,17},{17... | collective-permute-start | bytes 98312 | tf_op jit(solution)/shard_map/ppermute | solution.py:22
  140.7 6.7 %collective-permute-start.10 = (f32[2,32,1,128]{3,1,2,0:T(8,128)S(1)}, f32[2,32,1,128]{3,1,2,0:T(8,128)S(1)}, u32[]{:S(2)}, u32[]{:S(2)}) collective-permute-start(f32[2,32,1,128]{3,1,2,0:T(8,128)S(1)} %pad_maximum_fusion.67), channel_id=1, source_target_pairs={{0,1},{1,2},{2,3},{3,4},{4,5},{5,6},{6,7},{7,8},{8,9},{9,10},{10,1... | collective-permute-start | bytes 98312 | tf_op jit(solution)/shard_map/ppermute | solution.py:22
  148.8 5.8 %collective-permute-start.13 = (f32[2,32,1,128]{3,1,2,0:T(8,128)S(1)}, f32[2,32,1,128]{3,1,2,0:T(8,128)S(1)}, u32[]{:S(2)}, u32[]{:S(2)}) collective-permute-start(f32[2,32,1,128]{3,1,2,0:T(8,128)S(1)} %pad_maximum_fusion.70), channel_id=1, source_target_pairs={{1,0},{2,1},{3,2},{4,3},{5,4},{6,5},{7,6},{8,7},{9,8},{10,9},{11,1... | collective-permute-start | bytes 98312 | tf_op jit(solution)/shard_map/ppermute | solution.py:22
  150.7 4.7 collective-permute-start.12
  156.1 8.5 %collective-permute-start.14 = (f32[2,32,1,128]{3,1,2,0:T(8,128)S(1)}, f32[2,32,1,128]{3,1,2,0:T(8,128)S(1)}, u32[]{:S(2)}, u32[]{:S(2)}) collective-permute-start(f32[2,32,1,128]{3,1,2,0:T(8,128)S(1)} %pad_maximum_fusion.71), channel_id=1, source_target_pairs={{0,1},{1,2},{2,3},{3,4},{4,5},{5,6},{6,7},{7,8},{8,9},{9,10},{10,1... | collective-permute-start | bytes 98312 | tf_op jit(solution)/shard_map/ppermute | solution.py:22
  161.5 4.1 collective-permute-start.15
  173.1 157.1 %copy-start.37 = (f32[256,256]{1,0:T(8,128)S(1)}, f32[256,256]{1,0:T(8,128)}, u32[]{:S(2)}) copy-start(f32[256,256]{1,0:T(8,128)} %param.25) | copy-start | bytes 786436
  341.5 14.9 %copy-start.48 = (f32[1,32,1,128]{3,1,2,0:T(8,128)S(1)}, f32[1,32,1,128]{3,1,2,0:T(8,128)}, u32[]{:S(2)}) copy-start(f32[1,32,1,128]{3,1,2,0:T(8,128)} %copy-done.47) | copy-start | bytes 49156
  344.5 11.8 %collective-permute-start.21 = (f32[2,32,1,128]{3,1,2,0:T(8,128)S(1)}, f32[2,32,1,128]{3,1,2,0:T(8,128)S(1)}, u32[]{:S(2)}, u32[]{:S(2)}) collective-permute-start(f32[2,32,1,128]{3,1,2,0:T(8,128)S(1)} %pad_maximum_fusion.80), channel_id=1, source_target_pairs={{1,0},{2,1},{3,2},{4,3},{5,4},{6,5},{7,6},{8,7},{9,8},{10,9},{11,1... | collective-permute-start | bytes 98312 | tf_op jit(solution)/shard_map/ppermute | solution.py:22
  347.1 9.2 %collective-permute-start.20 = (f32[2,1,32,128]{3,2,1,0:T(8,128)}, f32[2,1,32,128]{3,2,1,0:T(8,128)S(1)}, u32[]{:S(2)}, u32[]{:S(2)}) collective-permute-start(f32[2,1,32,128]{3,2,1,0:T(8,128)} %pad_maximum_fusion.79), channel_id=1, source_target_pairs={{16,0},{32,16},{48,32},{64,48},{80,64},{96,80},{112,96},{17,1},{33... | collective-permute-start | bytes 98312 | tf_op jit(solution)/shard_map/ppermute | solution.py:22
  360.5 8.2 %collective-permute-start.23 = (f32[2,1,32,128]{3,2,1,0:T(8,128)S(1)}, f32[2,1,32,128]{3,2,1,0:T(8,128)S(1)}, u32[]{:S(2)}, u32[]{:S(2)}) collective-permute-start(f32[2,1,32,128]{3,2,1,0:T(8,128)S(1)} %pad_maximum_fusion.82), channel_id=1, source_target_pairs={{0,16},{16,32},{32,48},{48,64},{64,80},{80,96},{96,112},{1,17},{17... | collective-permute-start | bytes 98312 | tf_op jit(solution)/shard_map/ppermute | solution.py:22
  364.5 5.2 %collective-permute-start.22 = (f32[2,32,1,128]{3,1,2,0:T(8,128)S(1)}, f32[2,32,1,128]{3,1,2,0:T(8,128)S(1)}, u32[]{:S(2)}, u32[]{:S(2)}) collective-permute-start(f32[2,32,1,128]{3,1,2,0:T(8,128)S(1)} %pad_maximum_fusion.81), channel_id=1, source_target_pairs={{0,1},{1,2},{2,3},{3,4},{4,5},{5,6},{6,7},{7,8},{8,9},{9,10},{10,1... | collective-permute-start | bytes 98312 | tf_op jit(solution)/shard_map/ppermute | solution.py:22
  370.6 18.2 %copy-start.39 = (f32[32,32,1]{2,1,0:T(8,128)S(1)}, f32[32,32,1]{2,1,0:T(8,128)}, u32[]{:S(2)}) copy-start(f32[32,32,1]{2,1,0:T(8,128)} %copy.5002) | copy-start | bytes 12292
  370.6 18.2 %copy-start.40 = (f32[32,32,1]{2,1,0:T(8,128)S(1)}, f32[32,32,1]{2,1,0:T(8,128)}, u32[]{:S(2)}) copy-start(f32[32,32,1]{2,1,0:T(8,128)} %copy.5000) | copy-start | bytes 12292
  370.7 5.9 %collective-permute-start.25 = (f32[2,32,1,128]{3,1,2,0:T(8,128)S(1)}, f32[2,32,1,128]{3,1,2,0:T(8,128)S(1)}, u32[]{:S(2)}, u32[]{:S(2)}) collective-permute-start(f32[2,32,1,128]{3,1,2,0:T(8,128)S(1)} %pad_maximum_fusion.84), channel_id=1, source_target_pairs={{1,0},{2,1},{3,2},{4,3},{5,4},{6,5},{7,6},{8,7},{9,8},{10,9},{11,1... | collective-permute-start | bytes 98312 | tf_op jit(solution)/shard_map/ppermute | solution.py:22
  372.8 4.7 collective-permute-start.24
  378.1 9.7 %collective-permute-start.27 = (f32[2,1,32,128]{3,2,1,0:T(8,128)S(1)}, f32[2,1,32,128]{3,2,1,0:T(8,128)S(1)}, u32[]{:S(2)}, u32[]{:S(2)}) collective-permute-start(f32[2,1,32,128]{3,2,1,0:T(8,128)S(1)} %pad_maximum_fusion.86), channel_id=1, source_target_pairs={{0,16},{16,32},{32,48},{48,64},{64,80},{80,96},{96,112},{1,17},{17... | collective-permute-start | bytes 98312 | tf_op jit(solution)/shard_map/ppermute | solution.py:22
  382.2 6.7 %collective-permute-start.26 = (f32[2,32,1,128]{3,1,2,0:T(8,128)S(1)}, f32[2,32,1,128]{3,1,2,0:T(8,128)S(1)}, u32[]{:S(2)}, u32[]{:S(2)}) collective-permute-start(f32[2,32,1,128]{3,1,2,0:T(8,128)S(1)} %pad_maximum_fusion.85), channel_id=1, source_target_pairs={{0,1},{1,2},{2,3},{3,4},{4,5},{5,6},{6,7},{7,8},{8,9},{9,10},{10,1... | collective-permute-start | bytes 98312 | tf_op jit(solution)/shard_map/ppermute | solution.py:22
  389.8 5.8 %collective-permute-start.29 = (f32[2,32,1,128]{3,1,2,0:T(8,128)S(1)}, f32[2,32,1,128]{3,1,2,0:T(8,128)S(1)}, u32[]{:S(2)}, u32[]{:S(2)}) collective-permute-start(f32[2,32,1,128]{3,1,2,0:T(8,128)S(1)} %pad_maximum_fusion.88), channel_id=1, source_target_pairs={{1,0},{2,1},{3,2},{4,3},{5,4},{6,5},{7,6},{8,7},{9,8},{10,9},{11,1... | collective-permute-start | bytes 98312 | tf_op jit(solution)/shard_map/ppermute | solution.py:22
  391.7 4.7 collective-permute-start.28
  397.6 8.4 %collective-permute-start.31 = (f32[2,1,32,128]{3,2,1,0:T(8,128)S(1)}, f32[2,1,32,128]{3,2,1,0:T(8,128)S(1)}, u32[]{:S(2)}, u32[]{:S(2)}) collective-permute-start(f32[2,1,32,128]{3,2,1,0:T(8,128)S(1)} %pad_maximum_fusion.90), channel_id=1, source_target_pairs={{0,16},{16,32},{32,48},{48,64},{64,80},{80,96},{96,112},{1,17},{17... | collective-permute-start | bytes 98312 | tf_op jit(solution)/shard_map/ppermute | solution.py:22
  400.3 6.7 %collective-permute-start.30 = (f32[2,32,1,128]{3,1,2,0:T(8,128)S(1)}, f32[2,32,1,128]{3,1,2,0:T(8,128)S(1)}, u32[]{:S(2)}, u32[]{:S(2)}) collective-permute-start(f32[2,32,1,128]{3,1,2,0:T(8,128)S(1)} %pad_maximum_fusion.89), channel_id=1, source_target_pairs={{0,1},{1,2},{2,3},{3,4},{4,5},{5,6},{6,7},{7,8},{8,9},{9,10},{10,1... | collective-permute-start | bytes 98312 | tf_op jit(solution)/shard_map/ppermute | solution.py:22
  412.5 48.3 %copy-start.3 = (f32[32,32,128]{2,1,0:T(8,128)S(1)}, f32[32,32,128]{2,1,0:T(8,128)}, u32[]{:S(2)}) copy-start(f32[32,32,128]{2,1,0:T(8,128)} %copy-done.2) | copy-start | bytes 1572868
  441.0 30.0 %all-to-all-start.2 = ((f32[128,2,16]{2,1,0:T(2,128)}), f32[128,2,16]{2,1,0:T(2,128)S(1)}, u32[]{:S(2)}, u32[]{:S(2)}) async-start(f32[128,2,16]{2,1,0:T(2,128)} %reshape.462), calls=%async_computation.2 | async-start | bytes 262144 | tf_op jit(solution)/shard_map/all_to_all | solution.py:194
  (43 other events, 382.3 us)
Sparse Core Ops, SparseCore 0:
  173.2 156.9 all-reduce.44
where the time goes:
time: 481 us; the launch traced here: 479 us
  waiting for transfers between devices  189 us (39%)
  starting transfers between devices  135 us (28%)
  local copies, waits for them, and re-layouts  63.3 us (13%)
  other arithmetic  62.6 us (13%)
  between operations  16.2 us (3%)
  matrix products  13.1 us (3%)
    psum x1, waiting for transfers between devices, shards(): far_field = lax.psum(partial_far, ('gx', 'gy'))  152 us
    ppermute x32, starting transfers between devices, passed_along(): return lax.ppermute(shard, axis, pairs)  91.1 us
    unnamed x7, other arithmetic  33.4 us
    gather x1, local copies, waits for them, and re-layouts, shards(): picked = column_grad[cells_x, cells_y]  27.6 us
    ppermute x32, waiting for transfers between devices, passed_along(): return lax.ppermute(shard, axis, pairs)  21.6 us
    all_to_all x1, starting transfers between devices, shards(): lax.all_to_all(picked.reshape(devices, capacity, 16), ('gx', 'gy'), split...  19.8 us
    dot_general x16, matrix products, contract(): jnp.einsum(pattern, first_op, second_op, precision=lax.Precision.HIGHEST)  13.1 us
    all_to_all x1, starting transfers between devices, shards(): lax.all_to_all(packed_at.reshape(devices, capacity, 2), ('gx', 'gy'), spl...  12.4 us
  transfers between devices with their start and end apart: 36, of which 19 were waited for; matrix products, arithmetic and copies ran while one was open for 14% of the time, Pallas kernels for 0%

commit v1 on v0

--- a/solution.py
+++ b/solution.py
@@ -3,6 +3,7 @@
 import jax.numpy as jnp
 from jax import lax
 from jax.sharding import PartitionSpec as P
+from jax.lax import psum
 
 TILE = 32
 P_DEV = 128
@@ -165,7 +166,7 @@
     row_count = U // devices
     row_start = linear * row_count
     partial_far = project_forward(mon_re, mon_im, table_x, table_y, norm_scale)
-    far_field = lax.psum(partial_far, ("gx", "gy"))
+    far_field = psum(psum(partial_far, axis_name="gx"), axis_name="gy")
     mine_rows = lax.dynamic_slice_in_dim(far_field, row_start, row_count, 2)
     focal_power = jnp.sum(mine_rows * mine_rows, axis=(0, 1))
     weighted = jnp.stack([target * far_field[0], -(target * far_field[1])])

time: 481 us -> 555 us (1.15)
  waiting for transfers between devices: 189 us -> 262 us
    psum x1 -> x2, waiting for transfers between devices: 152 us -> 224 us  [shards(): far_field = psum(psum(partial_far, axis_name='gx'), axis_name='gy')]
  transfers between devices with their start and end apart: 36 -> 37, of which waited for: 19 -> 21; matrix products, arithmetic and copies ran while one was open for 14% -> 12% of each run, Pallas kernels for 0% -> 0%
where the time goes in v1:
time: 555 us; the launch traced here: 554 us
  waiting for transfers between devices  262 us (47%)
  starting transfers between devices  138 us (25%)
  local copies, waits for them, and re-layouts  62.7 us (11%)
  other arithmetic  61.4 us (11%)
  between operations  16.4 us (3%)
  matrix products  13.1 us (2%)
    psum x2, waiting for transfers between devices, shards(): far_field = psum(psum(partial_far, axis_name='gx'), axis_name='gy')  224 us
    ppermute x32, starting transfers between devices, passed_along(): return lax.ppermute(shard, axis, pairs)  91.6 us
    unnamed x7, other arithmetic  32.5 us
    gather x1, local copies, waits for them, and re-layouts, shards(): picked = column_grad[cells_x, cells_y]  27.6 us
    all_to_all x1, starting transfers between devices, shards(): lax.all_to_all(picked.reshape(devices, capacity, 16), ('gx', 'gy'), split...  22.3 us
    ppermute x32, waiting for transfers between devices, passed_along(): return lax.ppermute(shard, axis, pairs)  21.3 us
    dot_general x16, matrix products, contract(): jnp.einsum(pattern, first_op, second_op, precision=lax.Precision.HIGHEST)  13.1 us
    all_to_all x1, starting transfers between devices, shards(): lax.all_to_all(packed_at.reshape(devices, capacity, 2), ('gx', 'gy'), spl...  12.4 us
  transfers between devices with their start and end apart: 37, of which 21 were waited for; matrix products, arithmetic and copies ran while one was open for 12% of the time, Pallas kernels for 0%

profile of v1, /device:TPU:1, one launch (start us, length us, event | category | flops | bytes accessed | tf_op | source)
XLA Modules:
  0.0 553.7 jit_solution(7364321585917053926)
XLA Ops:
  9.9 3.3 collective-permute-start.17
  18.8 12.4 %all-to-all-start = ((f32[128,2,2]{1,2,0:T(2,128)}), f32[128,2,2]{1,2,0:T(2,128)S(1)}, u32[]{:S(2)}, u32[]{:S(2)}) async-start(f32[128,2,2]{1,2,0:T(2,128)} %copy.4958), calls=%async_computation | async-start | bytes 262144 | tf_op jit(solution)/shard_map/all_to_all | solution.py:127
  31.2 2.3 slice_bitcast_fusion.3
  35.1 3.0 collective-permute-start.1
  41.4 11.3 %all-to-all-start.1 = ((f32[128,2,16]{2,1,0:T(2,128)}), f32[128,2,16]{2,1,0:T(2,128)S(1)}, u32[]{:S(2)}, u32[]{:S(2)}) async-start(f32[128,2,16]{2,1,0:T(2,128)} %bitcast.24), calls=%async_computation.1 | async-start | bytes 262144 | tf_op jit(solution)/shard_map/all_to_all | solution.py:120
  54.1 8.7 %all-to-all-done.1 = f32[128,2,16]{2,1,0:T(2,128)S(1)} async-done(((f32[128,2,16]{2,1,0:T(2,128)}), f32[128,2,16]{2,1,0:T(2,128)S(1)}, u32[]{:S(2)}, u32[]{:S(2)}) %all-to-all-start.1) | async-done | bytes 16416 | tf_op jit(solution)/shard_map/all_to_all | solution.py:120
  63.0 28.8 %scatter_custom_fusion.2 = f32[1024]{0:T(1024)S(1)} fusion(s32[4096]{0:T(1024)S(1)} %reshape.500, f32[4096]{0:T(1024)S(1)} %reshape.502, f32[]{:T(128)} %constant.251.clone.1), kind=kCustom, calls=%fused_computation.635 | custom fusion | flops 4096 | bytes 4100
  94.1 2.7 collective-permute-start.18
  96.8 2.2 collective-permute-start.19
  99.8 3.5 collective-permute-start.3
  103.3 2.6 collective-permute-start.2
  109.7 1.9 collective-permute-start.5
  112.9 2.0 collective-permute-done.5
  116.9 3.1 collective-permute-start.7
  120.1 5.1 collective-permute-start.6
  127.6 1.9 collective-permute-start.9
  130.9 2.6 collective-permute-done.9
  134.8 2.7 collective-permute-start.11
  137.6 5.8 %collective-permute-start.10 = (f32[2,32,1,128]{3,1,2,0:T(8,128)S(1)}, f32[2,32,1,128]{3,1,2,0:T(8,128)S(1)}, u32[]{:S(2)}, u32[]{:S(2)}) collective-permute-start(f32[2,32,1,128]{3,1,2,0:T(8,128)S(1)} %pad_maximum_fusion.67), channel_id=1, source_target_pairs={{0,1},{1,2},{2,3},{3,4},{4,5},{5,6},{6,7},{7,8},{8,9},{9,10},{10,1... | collective-permute-start | bytes 98312 | tf_op jit(solution)/shard_map/ppermute | solution.py:23
  145.7 1.9 collective-permute-start.13
  149.0 2.6 collective-permute-done.13
  153.0 5.4 collective-permute-start.14
  158.4 3.1 collective-permute-start.15
  170.4 86.0 %all-reduce.46.cloned.1.call-done = f32[2,2,256,256]{3,2,1,0:T(8,128)} async-done(((f32[2,2,256,256]{3,2,1,0:T(8,128)}), f32[2,2,256,256]{3,2,1,0:T(8,128)}) %all-reduce.46.cloned.1.call-update) | async-done | bytes 1048592 | tf_op jit(solution)/shard_map/psum | solution.py:169
  259.7 3.1 bitcast_dynamic-update-slice_fusion.3
  264.4 138.1 %all-reduce.48.cloned.1.call-done = f32[2,2,256,256]{3,2,1,0:T(8,128)} async-done(((f32[2,2,256,256]{3,2,1,0:T(8,128)}), f32[2,2,256,256]{3,2,1,0:T(8,128)}) %all-reduce.48.cloned.1.call-update) | async-done | bytes 1048592 | tf_op jit(solution)/shard_map/psum | solution.py:169
  402.5 1.8 fusion.284
  404.3 1.8 convolution_add_fusion.2
  406.5 1.8 fusion.286
  408.3 1.8 convolution_subtract_fusion.2
  413.8 3.0 fusion.94
  416.8 2.8 collective-permute-start.21
  428.8 3.9 fusion.98
  432.8 4.0 collective-permute-start.23
  436.8 3.4 collective-permute-start.22
  442.2 2.1 collective-permute-start.25
  445.6 2.6 collective-permute-done.25
  449.6 4.0 collective-permute-start.27
  453.6 5.7 %collective-permute-start.26 = (f32[2,32,1,128]{3,1,2,0:T(8,128)S(1)}, f32[2,32,1,128]{3,1,2,0:T(8,128)S(1)}, u32[]{:S(2)}, u32[]{:S(2)}) collective-permute-start(f32[2,32,1,128]{3,1,2,0:T(8,128)S(1)} %pad_maximum_fusion.85), channel_id=1, source_target_pairs={{0,1},{1,2},{2,3},{3,4},{4,5},{5,6},{6,7},{7,8},{8,9},{9,10},{10,1... | collective-permute-start | bytes 98312 | tf_op jit(solution)/shard_map/ppermute | solution.py:23
  461.2 1.9 collective-permute-start.29
  463.1 1.6 collective-permute-start.28
  464.7 2.3 collective-permute-done.29
  469.0 3.3 collective-permute-start.31
  472.3 5.7 %collective-permute-start.30 = (f32[2,32,1,128]{3,1,2,0:T(8,128)S(1)}, f32[2,32,1,128]{3,1,2,0:T(8,128)S(1)}, u32[]{:S(2)}, u32[]{:S(2)}) collective-permute-start(f32[2,32,1,128]{3,1,2,0:T(8,128)S(1)} %pad_maximum_fusion.89), channel_id=1, source_target_pairs={{0,1},{1,2},{2,3},{3,4},{4,5},{5,6},{6,7},{7,8},{8,9},{9,10},{10,1... | collective-permute-start | bytes 98312 | tf_op jit(solution)/shard_map/ppermute | solution.py:23
  479.1 5.4 fusion.147
  484.6 27.6 %gather_fusion = f32[4096]{0:T(1024)S(1)} fusion(f32[32,32]{0,1:T(8,128)S(1)} %copy.5037, s32[4096]{0:T(1024)S(1)} %reshape.470), kind=kCustom, calls=%fused_computation | custom fusion | bytes 65536 | tf_op jit(solution)/shard_map/gather | solution.py:194
  513.0 22.3 %all-to-all-start.2 = ((f32[128,2,16]{2,1,0:T(2,128)}), f32[128,2,16]{2,1,0:T(2,128)S(1)}, u32[]{:S(2)}, u32[]{:S(2)}) async-start(f32[128,2,16]{2,1,0:T(2,128)} %reshape.462), calls=%async_computation.2 | async-start | bytes 262144 | tf_op jit(solution)/shard_map/all_to_all | solution.py:195
  537.5 7.9 %all-to-all-done.2 = f32[128,2,16]{2,1,0:T(2,128)S(1)} async-done(((f32[128,2,16]{2,1,0:T(2,128)}), f32[128,2,16]{2,1,0:T(2,128)S(1)}, u32[]{:S(2)}, u32[]{:S(2)}) %all-to-all-start.2) | async-done | bytes 16416 | tf_op jit(solution)/shard_map/all_to_all | solution.py:195
  (395 shorter events, 75.0 us)
Async XLA Ops:
  7.8 84.0 %collective-permute-start.16 = (f32[2,1,32,128]{3,2,1,0:T(8,128)}, f32[2,1,32,128]{3,2,1,0:T(8,128)}, u32[]{:S(2)}, u32[]{:S(2)}) collective-permute-start(f32[2,1,32,128]{3,2,1,0:T(8,128)} %stack.374), channel_id=1, source_target_pairs={{16,0},{32,16},{48,32},{64,48},{80,64},{96,80},{112,96},{17,1},{33... | collective-permute-start | bytes 98312 | tf_op jit(solution)/shard_map/ppermute | solution.py:23
  9.9 82.9 %collective-permute-start.17 = (f32[2,32,1,128]{3,1,2,0:T(8,128)}, f32[2,32,1,128]{3,1,2,0:T(8,128)}, u32[]{:S(2)}, u32[]{:S(2)}) collective-permute-start(f32[2,32,1,128]{3,1,2,0:T(8,128)} %stack.375), channel_id=1, source_target_pairs={{1,0},{2,1},{3,2},{4,3},{5,4},{6,5},{7,6},{8,7},{9,8},{10,9},{11,1... | collective-permute-start | bytes 98312 | tf_op jit(solution)/shard_map/ppermute | solution.py:23
  18.8 22.5 %all-to-all-start = ((f32[128,2,2]{1,2,0:T(2,128)}), f32[128,2,2]{1,2,0:T(2,128)S(1)}, u32[]{:S(2)}, u32[]{:S(2)}) async-start(f32[128,2,2]{1,2,0:T(2,128)} %copy.4958), calls=%async_computation | async-start | bytes 262144 | tf_op jit(solution)/shard_map/all_to_all | solution.py:127
  35.1 63.9 %collective-permute-start.1 = (f32[2,32,1,128]{3,1,2,0:T(8,128)}, f32[2,32,1,128]{3,1,2,0:T(8,128)S(1)}, u32[]{:S(2)}, u32[]{:S(2)}) collective-permute-start(f32[2,32,1,128]{3,1,2,0:T(8,128)} %pad_maximum_fusion.58), channel_id=1, source_target_pairs={{1,0},{2,1},{3,2},{4,3},{5,4},{6,5},{7,6},{8,7},{9,8},{10,9},{11,1... | collective-permute-start | bytes 98312 | tf_op jit(solution)/shard_map/ppermute | solution.py:23
  38.1 60.9 %collective-permute-start = (f32[2,1,32,128]{3,2,1,0:T(8,128)S(1)}, f32[2,1,32,128]{3,2,1,0:T(8,128)S(1)}, u32[]{:S(2)}, u32[]{:S(2)}) collective-permute-start(f32[2,1,32,128]{3,2,1,0:T(8,128)S(1)} %stack.314), channel_id=1, source_target_pairs={{16,0},{32,16},{48,32},{64,48},{80,64},{96,80},{112,96},{17,1},{33... | collective-permute-start | bytes 98312 | tf_op jit(solution)/shard_map/ppermute | solution.py:23
  39.5 128.7 %copy-start.47 = (f32[256]{0:T(256)}, f32[256]{0:T(256)S(1)}, u32[]{:S(2)}) copy-start(f32[256]{0:T(256)S(1)} %multiply_add_fusion.1) | copy-start | bytes 3076
  39.5 127.5 %copy-start.61 = (f32[32]{0:T(128)}, f32[32]{0:T(128)S(1)}, u32[]{:S(2)}) copy-start(f32[32]{0:T(128)S(1)} %multiply_add_fusion.3) | copy-start | bytes 388
  39.6 128.6 %copy-start.64 = (f32[32]{0:T(128)}, f32[32]{0:T(128)S(1)}, u32[]{:S(2)}) copy-start(f32[32]{0:T(128)S(1)} %multiply_add_fusion.2) | copy-start | bytes 388
  41.4 21.4 %all-to-all-start.1 = ((f32[128,2,16]{2,1,0:T(2,128)}), f32[128,2,16]{2,1,0:T(2,128)S(1)}, u32[]{:S(2)}, u32[]{:S(2)}) async-start(f32[128,2,16]{2,1,0:T(2,128)} %bitcast.24), calls=%async_computation.1 | async-start | bytes 262144 | tf_op jit(solution)/shard_map/all_to_all | solution.py:120
  52.7 203.7 %all-reduce.46.cloned.1.call-start = ((), (), s32[]{:S(2)}) async-start(), calls=%async_computation.3 | async-start | bytes 2097152 | tf_op jit(solution)/shard_map/psum | solution.py:169
  94.1 11.9 %collective-permute-start.18 = (f32[2,32,1,128]{3,1,2,0:T(8,128)S(1)}, f32[2,32,1,128]{3,1,2,0:T(8,128)S(1)}, u32[]{:S(2)}, u32[]{:S(2)}) collective-permute-start(f32[2,32,1,128]{3,1,2,0:T(8,128)S(1)} %pad_maximum_fusion.77), channel_id=1, source_target_pairs={{0,1},{1,2},{2,3},{3,4},{4,5},{5,6},{6,7},{7,8},{8,9},{9,10},{10,1... | collective-permute-start | bytes 98312 | tf_op jit(solution)/shard_map/ppermute | solution.py:23
  96.8 9.8 %collective-permute-start.19 = (f32[2,1,32,128]{3,2,1,0:T(8,128)S(1)}, f32[2,1,32,128]{3,2,1,0:T(8,128)S(1)}, u32[]{:S(2)}, u32[]{:S(2)}) collective-permute-start(f32[2,1,32,128]{3,2,1,0:T(8,128)S(1)} %pad_maximum_fusion.78), channel_id=1, source_target_pairs={{0,16},{16,32},{32,48},{48,64},{64,80},{80,96},{96,112},{1,17},{17... | collective-permute-start | bytes 98312 | tf_op jit(solution)/shard_map/ppermute | solution.py:23
  99.8 8.4 %collective-permute-start.3 = (f32[2,1,32,128]{3,2,1,0:T(8,128)S(1)}, f32[2,1,32,128]{3,2,1,0:T(8,128)S(1)}, u32[]{:S(2)}, u32[]{:S(2)}) collective-permute-start(f32[2,1,32,128]{3,2,1,0:T(8,128)S(1)} %pad_maximum_fusion.60), channel_id=1, source_target_pairs={{0,16},{16,32},{32,48},{48,64},{64,80},{80,96},{96,112},{1,17},{17... | collective-permute-start | bytes 98312 | tf_op jit(solution)/shard_map/ppermute | solution.py:23
  103.3 4.9 collective-permute-start.2
  109.7 5.2 collective-permute-start.5
  111.6 4.7 collective-permute-start.4
  116.9 8.2 %collective-permute-start.7 = (f32[2,1,32,128]{3,2,1,0:T(8,128)S(1)}, f32[2,1,32,128]{3,2,1,0:T(8,128)S(1)}, u32[]{:S(2)}, u32[]{:S(2)}) collective-permute-start(f32[2,1,32,128]{3,2,1,0:T(8,128)S(1)} %pad_maximum_fusion.64), channel_id=1, source_target_pairs={{0,16},{16,32},{32,48},{48,64},{64,80},{80,96},{96,112},{1,17},{17... | collective-permute-start | bytes 98312 | tf_op jit(solution)/shard_map/ppermute | solution.py:23
  120.1 6.1 %collective-permute-start.6 = (f32[2,32,1,128]{3,1,2,0:T(8,128)S(1)}, f32[2,32,1,128]{3,1,2,0:T(8,128)S(1)}, u32[]{:S(2)}, u32[]{:S(2)}) collective-permute-start(f32[2,32,1,128]{3,1,2,0:T(8,128)S(1)} %pad_maximum_fusion.63), channel_id=1, source_target_pairs={{0,1},{1,2},{2,3},{3,4},{4,5},{5,6},{6,7},{7,8},{8,9},{9,10},{10,1... | collective-permute-start | bytes 98312 | tf_op jit(solution)/shard_map/ppermute | solution.py:23
  127.6 5.8 %collective-permute-start.9 = (f32[2,32,1,128]{3,1,2,0:T(8,128)S(1)}, f32[2,32,1,128]{3,1,2,0:T(8,128)S(1)}, u32[]{:S(2)}, u32[]{:S(2)}) collective-permute-start(f32[2,32,1,128]{3,1,2,0:T(8,128)S(1)} %pad_maximum_fusion.66), channel_id=1, source_target_pairs={{1,0},{2,1},{3,2},{4,3},{5,4},{6,5},{7,6},{8,7},{9,8},{10,9},{11,1... | collective-permute-start | bytes 98312 | tf_op jit(solution)/shard_map/ppermute | solution.py:23
  129.6 4.7 collective-permute-start.8
  134.8 8.6 %collective-permute-start.11 = (f32[2,1,32,128]{3,2,1,0:T(8,128)S(1)}, f32[2,1,32,128]{3,2,1,0:T(8,128)S(1)}, u32[]{:S(2)}, u32[]{:S(2)}) collective-permute-start(f32[2,1,32,128]{3,2,1,0:T(8,128)S(1)} %pad_maximum_fusion.68), channel_id=1, source_target_pairs={{0,16},{16,32},{32,48},{48,64},{64,80},{80,96},{96,112},{1,17},{17... | collective-permute-start | bytes 98312 | tf_op jit(solution)/shard_map/ppermute | solution.py:23
  137.6 6.7 %collective-permute-start.10 = (f32[2,32,1,128]{3,1,2,0:T(8,128)S(1)}, f32[2,32,1,128]{3,1,2,0:T(8,128)S(1)}, u32[]{:S(2)}, u32[]{:S(2)}) collective-permute-start(f32[2,32,1,128]{3,1,2,0:T(8,128)S(1)} %pad_maximum_fusion.67), channel_id=1, source_target_pairs={{0,1},{1,2},{2,3},{3,4},{4,5},{5,6},{6,7},{7,8},{8,9},{9,10},{10,1... | collective-permute-start | bytes 98312 | tf_op jit(solution)/shard_map/ppermute | solution.py:23
  145.7 5.8 %collective-permute-start.13 = (f32[2,32,1,128]{3,1,2,0:T(8,128)S(1)}, f32[2,32,1,128]{3,1,2,0:T(8,128)S(1)}, u32[]{:S(2)}, u32[]{:S(2)}) collective-permute-start(f32[2,32,1,128]{3,1,2,0:T(8,128)S(1)} %pad_maximum_fusion.70), channel_id=1, source_target_pairs={{1,0},{2,1},{3,2},{4,3},{5,4},{6,5},{7,6},{8,7},{9,8},{10,9},{11,1... | collective-permute-start | bytes 98312 | tf_op jit(solution)/shard_map/ppermute | solution.py:23
  147.7 4.7 collective-permute-start.12
  153.0 8.5 %collective-permute-start.14 = (f32[2,32,1,128]{3,1,2,0:T(8,128)S(1)}, f32[2,32,1,128]{3,1,2,0:T(8,128)S(1)}, u32[]{:S(2)}, u32[]{:S(2)}) collective-permute-start(f32[2,32,1,128]{3,1,2,0:T(8,128)S(1)} %pad_maximum_fusion.71), channel_id=1, source_target_pairs={{0,1},{1,2},{2,3},{3,4},{4,5},{5,6},{6,7},{7,8},{8,9},{9,10},{10,1... | collective-permute-start | bytes 98312 | tf_op jit(solution)/shard_map/ppermute | solution.py:23
  158.4 4.1 collective-permute-start.15
  167.4 89.0 %copy-start.69 = (s32[128]{0:T(128)S(1)}, s32[128]{0:T(128)}, u32[]{:S(2)}) copy-start(s32[128]{0:T(128)} %copy-done.68) | copy-start | bytes 1540
  167.4 90.3 %copy-start.60 = (s32[256,16,1]{0,1,2:T(8,128)S(1)}, s32[256,16,1]{0,1,2:T(8,128)}, u32[]{:S(2)}) copy-start(s32[256,16,1]{0,1,2:T(8,128)} %get-tuple-element.260) | copy-start | bytes 49156
  170.1 232.4 %all-reduce.48.cloned.1.call-start = ((), (), s32[]{:S(2)}) async-start(), calls=%async_computation.4 | async-start | bytes 2097152 | tf_op jit(solution)/shard_map/psum | solution.py:169
  256.4 146.2 %copy-start.36 = (f32[256,256]{1,0:T(8,128)S(1)}, f32[256,256]{1,0:T(8,128)}, u32[]{:S(2)}) copy-start(f32[256,256]{1,0:T(8,128)} %param.25) | copy-start | bytes 786436
  257.9 144.6 %copy-start.48 = (f32[256]{0:T(256)S(1)}, f32[256]{0:T(256)}, u32[]{:S(2)}) copy-start(f32[256]{0:T(256)} %copy-done.47) | copy-start | bytes 3076
  257.9 144.6 %copy-start.65 = (f32[32]{0:T(128)S(1)}, f32[32]{0:T(128)}, u32[]{:S(2)}) copy-start(f32[32]{0:T(128)} %copy-done.64) | copy-start | bytes 388
  259.7 146.4 %copy-start.62 = (f32[32]{0:T(128)S(1)}, f32[32]{0:T(128)}, u32[]{:S(2)}) copy-start(f32[32]{0:T(128)} %copy-done.61) | copy-start | bytes 388
  263.6 150.2 %copy-start.58 = (f32[1,32,1,128]{3,1,2,0:T(8,128)S(1)}, f32[1,32,1,128]{3,1,2,0:T(8,128)}, u32[]{:S(2)}) copy-start(f32[1,32,1,128]{3,1,2,0:T(8,128)} %get-tuple-element.220) | copy-start | bytes 49156
  263.6 150.2 %copy-start.59 = (f32[1,32,128]{2,1,0:T(8,128)S(1)}, f32[1,32,128]{2,1,0:T(8,128)}, u32[]{:S(2)}) copy-start(f32[1,32,128]{2,1,0:T(8,128)} %get-tuple-element.218) | copy-start | bytes 49156
  416.8 11.8 %collective-permute-start.21 = (f32[2,32,1,128]{3,1,2,0:T(8,128)S(1)}, f32[2,32,1,128]{3,1,2,0:T(8,128)S(1)}, u32[]{:S(2)}, u32[]{:S(2)}) collective-permute-start(f32[2,32,1,128]{3,1,2,0:T(8,128)S(1)} %pad_maximum_fusion.80), channel_id=1, source_target_pairs={{1,0},{2,1},{3,2},{4,3},{5,4},{6,5},{7,6},{8,7},{9,8},{10,9},{11,1... | collective-permute-start | bytes 98312 | tf_op jit(solution)/shard_map/ppermute | solution.py:23
  419.6 9.1 %collective-permute-start.20 = (f32[2,1,32,128]{3,2,1,0:T(8,128)S(1)}, f32[2,1,32,128]{3,2,1,0:T(8,128)S(1)}, u32[]{:S(2)}, u32[]{:S(2)}) collective-permute-start(f32[2,1,32,128]{3,2,1,0:T(8,128)S(1)} %pad_maximum_fusion.79), channel_id=1, source_target_pairs={{16,0},{32,16},{48,32},{64,48},{80,64},{96,80},{112,96},{17,1},{33... | collective-permute-start | bytes 98312 | tf_op jit(solution)/shard_map/ppermute | solution.py:23
  432.8 7.4 %collective-permute-start.23 = (f32[2,1,32,128]{3,2,1,0:T(8,128)S(1)}, f32[2,1,32,128]{3,2,1,0:T(8,128)S(1)}, u32[]{:S(2)}, u32[]{:S(2)}) collective-permute-start(f32[2,1,32,128]{3,2,1,0:T(8,128)S(1)} %pad_maximum_fusion.82), channel_id=1, source_target_pairs={{0,16},{16,32},{32,48},{48,64},{64,80},{80,96},{96,112},{1,17},{17... | collective-permute-start | bytes 98312 | tf_op jit(solution)/shard_map/ppermute | solution.py:23
  436.8 4.4 collective-permute-start.22
  442.2 5.9 %collective-permute-start.25 = (f32[2,32,1,128]{3,1,2,0:T(8,128)S(1)}, f32[2,32,1,128]{3,1,2,0:T(8,128)S(1)}, u32[]{:S(2)}, u32[]{:S(2)}) collective-permute-start(f32[2,32,1,128]{3,1,2,0:T(8,128)S(1)} %pad_maximum_fusion.84), channel_id=1, source_target_pairs={{1,0},{2,1},{3,2},{4,3},{5,4},{6,5},{7,6},{8,7},{9,8},{10,9},{11,1... | collective-permute-start | bytes 98312 | tf_op jit(solution)/shard_map/ppermute | solution.py:23
  444.3 4.7 collective-permute-start.24
  449.6 9.7 %collective-permute-start.27 = (f32[2,1,32,128]{3,2,1,0:T(8,128)S(1)}, f32[2,1,32,128]{3,2,1,0:T(8,128)S(1)}, u32[]{:S(2)}, u32[]{:S(2)}) collective-permute-start(f32[2,1,32,128]{3,2,1,0:T(8,128)S(1)} %pad_maximum_fusion.86), channel_id=1, source_target_pairs={{0,16},{16,32},{32,48},{48,64},{64,80},{80,96},{96,112},{1,17},{17... | collective-permute-start | bytes 98312 | tf_op jit(solution)/shard_map/ppermute | solution.py:23
  453.6 6.7 %collective-permute-start.26 = (f32[2,32,1,128]{3,1,2,0:T(8,128)S(1)}, f32[2,32,1,128]{3,1,2,0:T(8,128)S(1)}, u32[]{:S(2)}, u32[]{:S(2)}) collective-permute-start(f32[2,32,1,128]{3,1,2,0:T(8,128)S(1)} %pad_maximum_fusion.85), channel_id=1, source_target_pairs={{0,1},{1,2},{2,3},{3,4},{4,5},{5,6},{6,7},{7,8},{8,9},{9,10},{10,1... | collective-permute-start | bytes 98312 | tf_op jit(solution)/shard_map/ppermute | solution.py:23
  461.2 5.8 %collective-permute-start.29 = (f32[2,32,1,128]{3,1,2,0:T(8,128)S(1)}, f32[2,32,1,128]{3,1,2,0:T(8,128)S(1)}, u32[]{:S(2)}, u32[]{:S(2)}) collective-permute-start(f32[2,32,1,128]{3,1,2,0:T(8,128)S(1)} %pad_maximum_fusion.88), channel_id=1, source_target_pairs={{1,0},{2,1},{3,2},{4,3},{5,4},{6,5},{7,6},{8,7},{9,8},{10,9},{11,1... | collective-permute-start | bytes 98312 | tf_op jit(solution)/shard_map/ppermute | solution.py:23
  463.1 4.7 collective-permute-start.28
  469.0 9.0 %collective-permute-start.31 = (f32[2,1,32,128]{3,2,1,0:T(8,128)S(1)}, f32[2,1,32,128]{3,2,1,0:T(8,128)S(1)}, u32[]{:S(2)}, u32[]{:S(2)}) collective-permute-start(f32[2,1,32,128]{3,2,1,0:T(8,128)S(1)} %pad_maximum_fusion.90), channel_id=1, source_target_pairs={{0,16},{16,32},{32,48},{48,64},{64,80},{80,96},{96,112},{1,17},{17... | collective-permute-start | bytes 98312 | tf_op jit(solution)/shard_map/ppermute | solution.py:23
  472.3 6.7 %collective-permute-start.30 = (f32[2,32,1,128]{3,1,2,0:T(8,128)S(1)}, f32[2,32,1,128]{3,1,2,0:T(8,128)S(1)}, u32[]{:S(2)}, u32[]{:S(2)}) collective-permute-start(f32[2,32,1,128]{3,1,2,0:T(8,128)S(1)} %pad_maximum_fusion.89), channel_id=1, source_target_pairs={{0,1},{1,2},{2,3},{3,4},{4,5},{5,6},{6,7},{7,8},{8,9},{9,10},{10,1... | collective-permute-start | bytes 98312 | tf_op jit(solution)/shard_map/ppermute | solution.py:23
  513.0 32.4 %all-to-all-start.2 = ((f32[128,2,16]{2,1,0:T(2,128)}), f32[128,2,16]{2,1,0:T(2,128)S(1)}, u32[]{:S(2)}, u32[]{:S(2)}) async-start(f32[128,2,16]{2,1,0:T(2,128)} %reshape.462), calls=%async_computation.2 | async-start | bytes 262144 | tf_op jit(solution)/shard_map/all_to_all | solution.py:195
  (59 other events, 810.5 us)
Sparse Core Ops, SparseCore 0:
  170.2 86.0 all-reduce.45
  258.8 143.6 all-reduce.47
